TPU v7x, 512 devices: a whole 4x4x16 slice. The times are simulated.
512 devices in a mesh: rows: 32 (over y_lo, z), filt: 16 (over y_hi, x, core).
Axes of the slice: x: 4, y: 4 (y_hi: 2, y_lo: 2; y = y_hi * 2 + y_lo), z: 16, core: 2. Of those that a mesh axis runs over, the one named last changes fastest.
Arguments:
- features: bfloat16 [512, 32, 512], P('filt', 'rows'), may hold values from -6 to 6
- first_weight: bfloat16 [512, 3, 3, 512], P('filt'), may hold values from -0.09375 to 0.09375
- second_weight: bfloat16 [512, 3, 3, 512], P('filt'), may hold values from -0.09375 to 0.09375
- out_grad: bfloat16 [512, 32, 512], P('filt', 'rows'), may hold values from -0.046875 to 0.046875
Outputs:
- block_out: bfloat16 [512, 32, 512], P('filt', 'rows')
- first_grad: float32 [512, 3, 3, 512], P('filt')
- second_grad: float32 [512, 3, 3, 512], P('filt')
All inputs are finite; a program needn't handle non-finite values.
Results may differ from a plain program's by a relative error of at most 0.024.
The roundings to bfloat16 on the way count: a program that leaves them out, or rounds other values in their place, can miss the bound.
Values may be sent and summed in bfloat16 or wider, within the bound.
A program may use at most 64 MiB of HBM per device.

v0:
```python
import jax
import jax.numpy as jnp
from jax import lax
from jax.sharding import PartitionSpec as P


def extended(cells, sides, width):
    for axis, dim in sides:
        count = lax.axis_size(axis)
        ends = count - 1
        head = lax.slice_in_dim(cells, 0, width, axis=dim)
        tail = lax.slice_in_dim(cells, cells.shape[dim] - width, cells.shape[dim], axis=dim)
        cells = jnp.concatenate(
            [
                lax.ppermute(tail, axis, [(i, (i + 1) % count) for i in range(ends)]),
                cells,
                lax.ppermute(head, axis, [((i + 1) % count, i) for i in range(ends)]),
            ],
            axis=dim,
        )
    return cells


def shift_cols(value, offset):
    if offset == 0:
        return value
    if offset > 0:
        return jnp.pad(value[..., offset:], ((0, 0), (0, 0), (0, offset)))
    return jnp.pad(value[..., :offset], ((0, 0), (0, 0), (-offset, 0)))


def conv_forward(weight, padded, count):
    total = jnp.zeros((weight.shape[0], count, padded.shape[2]), jnp.float32)
    for a in range(3):
        for b in range(3):
            part = jnp.einsum(
                "oi,ihw->ohw",
                weight[:, a, b, :],
                padded[:, a : a + count, :],
                preferred_element_type=jnp.float32,
            )
            total = total + shift_cols(part, b - 1)
    return total


def conv_backward(weight, padded, count):
    total = jnp.zeros((weight.shape[3], count, padded.shape[2]), jnp.float32)
    for a in range(3):
        for b in range(3):
            part = jnp.einsum(
                "oi,ohw->ihw",
                weight[:, a, b, :],
                padded[:, 2 - a : 2 - a + count, :],
                preferred_element_type=jnp.float32,
            )
            total = total + shift_cols(part, 1 - b)
    return total


def weight_terms(grad, padded, count):
    rows_out = []
    for a in range(3):
        cols_out = []
        for b in range(3):
            moved = shift_cols(grad, 1 - b)
            cols_out.append(
                jnp.einsum(
                    "ohw,ihw->oi",
                    moved,
                    padded[:, a : a + count, :],
                    preferred_element_type=jnp.float32,
                )
            )
        rows_out.append(jnp.stack(cols_out, axis=1))
    return jnp.stack(rows_out, axis=1)


def with_rims(value):
    return extended(value, (("rows", 1),), 1)


def all_channels(value):
    return lax.all_gather(with_rims(value), "filt", axis=0, tiled=True)


def per_device(features, first_weight, second_weight, out_grad):
    count = features.shape[1]
    padded_in = all_channels(features)
    pre_first = conv_forward(first_weight, padded_in, count)
    hidden = jnp.maximum(pre_first, 0.0).astype(jnp.bfloat16)
    padded_hidden = all_channels(hidden)
    pre_second = conv_forward(second_weight, padded_hidden, count) + features.astype(jnp.float32)
    block_out = jnp.maximum(pre_second, 0.0).astype(jnp.bfloat16)
    grad_second = jnp.where(pre_second > 0, out_grad.astype(jnp.float32), 0.0).astype(jnp.bfloat16)
    rimmed_grad = with_rims(grad_second)
    terms = conv_backward(second_weight, rimmed_grad, count)
    hidden_grad = lax.psum_scatter(terms, "filt", scatter_dimension=0, tiled=True)
    grad_first = jnp.where(pre_first > 0, hidden_grad, 0.0).astype(jnp.bfloat16)
    second_local = weight_terms(grad_second, padded_hidden, count)
    first_local = weight_terms(grad_first, padded_in, count)
    first_grad, second_grad = lax.psum((first_local, second_local), "rows")
    return (block_out, first_grad, second_grad)


def solution(mesh):
    in_specs = (
        P("filt", "rows", None),
        P("filt", None, None, None),
        P("filt", None, None, None),
        P("filt", "rows", None),
    )
    out_specs = (P("filt", "rows", None), P("filt", None, None, None), P("filt", None, None, None))
    return jax.shard_map(
        per_device, mesh=mesh, in_specs=in_specs, out_specs=out_specs, check_vma=False
    )
```

profile of v0, /device:TPU:2, one launch (start us, length us, event | category | flops | bytes accessed | tf_op | source)
XLA Modules:
  0.0 543.7 jit_solution(2598938622587336115)
XLA Ops:
  7.2 4.0 collective-permute-start
  11.2 1.3 collective-permute-start.1
  12.5 0.6 collective-permute-done
  13.1 4.1 collective-permute-done.1
  17.2 1.4 pad_maximum_fusion.2
  18.7 66.2 %all-gather.3.cloned.1.call-done = bf16[512,3,512]{2,0,1:T(8,128)(2,1)} async-done(((bf16[32,3,512]{2,0,1:T(8,128)(2,1)}), bf16[512,3,512]{2,0,1:T(8,128)(2,1)}) %all-gather.3.cloned.1.call-update) | async-done | bytes 1572880 | tf_op jit(solution)/shard_map/all_gather | solution.py:83
  84.9 1.4 convolution_bitcast_fusion.24
  86.4 1.3 convolution_bitcast_fusion.21
  87.7 1.2 convolution_bitcast_fusion.18
  90.1 0.8 maximum_convert_fusion.1
  90.9 3.4 collective-permute-start.2
  94.4 1.3 collective-permute-start.3
  95.7 0.3 collective-permute-done.2
  96.0 4.2 collective-permute-done.3
  100.2 0.7 pad_maximum_fusion.3
  100.9 61.3 %all-gather.5.cloned.1.call-done = bf16[512,3,512]{2,0,1:T(8,128)(2,1)} async-done(((bf16[32,3,512]{2,0,1:T(8,128)(2,1)}), bf16[512,3,512]{2,0,1:T(8,128)(2,1)}) %all-gather.5.cloned.1.call-update) | async-done | bytes 1572880 | tf_op jit(solution)/shard_map/all_gather | solution.py:83
  162.2 1.3 convolution_bitcast_fusion.15
  163.7 1.2 convolution_bitcast_fusion.12
  165.0 1.2 convolution_bitcast_fusion.9
  167.4 0.8 maximum_convert_fusion
  168.3 1.3 collective-permute-start.4
  169.6 4.5 collective-permute-start.5
  174.1 0.3 convolution_bitcast_fusion.5
  174.5 0.3 convolution_bitcast_fusion.3
  174.8 0.3 convolution_bitcast_fusion.4
  175.2 0.3 slice.251
  175.5 0.3 convolution_bitcast_fusion.8
  175.9 0.3 slice.249
  176.2 0.3 convolution_bitcast_fusion.2
  176.6 0.3 slice.253
  176.9 0.3 convolution_bitcast_fusion
  177.2 0.3 convolution_bitcast_fusion.6
  177.6 0.3 convolution_bitcast_fusion.7
  177.9 2.0 fusion.1
  180.3 0.3 convolution_bitcast_fusion.29
  180.5 0.3 convolution_bitcast_fusion.28
  181.1 0.3 convolution_bitcast_fusion.32
  181.6 0.3 convolution_bitcast_fusion.35
  182.5 0.9 pad_maximum_fusion.1
  183.4 87.0 %reduce-scatter.2.cloned.1.call-done = f32[32,1,512]{2,0,1:T(8,128)} async-done(((f32[512,1,512]{2,0,1:T(8,128)}), f32[32,1,512]{2,0,1:T(8,128)}) %reduce-scatter.2.cloned.1.call-update) | async-done | bytes 65552 | tf_op jit(solution)/shard_map/reduce_scatter | solution.py:97
  270.4 0.8 select_convert_fusion
  271.6 0.3 convolution_bitcast_fusion.38
  272.4 0.3 convolution_bitcast_fusion.41
  272.9 0.3 convolution_bitcast_fusion.44
  273.8 0.9 pad_maximum_fusion
  274.7 259.7 %all-reduce.25.cloned.1.call-done = (f32[32,3,3,512]{3,0,2,1:T(8,128)}, f32[32,3,3,512]{3,0,2,1:T(8,128)}) async-done(((f32[32,3,3,512]{3,0,2,1:T(8,128)}, f32[32,3,3,512]{3,0,2,1:T(8,128)}), (f32[32,3,3,512]{3,0,2,1:T(8,128)}, f32[32,3,3,512]{3,0,2,1:T(8,128)})) %all-reduce.25.cloned.1.call-update) | async-done | bytes 1179664 | tf_op jit(solution)/shard_map/psum | solution.py:101
  534.3 2.0 copy.27
  536.3 0.8 copy.28
  (60 shorter events, 5.9 us)
Async XLA Ops:
  7.2 80.6 %copy-start.4 = (bf16[32,3,3,512]{3,0,2,1:T(8,128)(2,1)S(1)}, bf16[32,3,3,512]{3,0,2,1:T(8,128)(2,1)}, u32[]{:S(2)}) copy-start(bf16[32,3,3,512]{3,0,2,1:T(8,128)(2,1)} %param.5) | copy-start | bytes 884740
  7.2 77.8 %all-gather.3.cloned.1.call-start = ((), (), s32[]{:S(2)}) async-start(), calls=%async_computation.1 | async-start | bytes 1671168 | tf_op jit(solution)/shard_map/all_gather | solution.py:83
  7.2 5.9 %collective-permute-start = (bf16[32,1,512]{2,0,1:T(8,128)(2,1)}, bf16[32,1,512]{2,0,1:T(8,128)(2,1)S(1)}, u32[]{:S(2)}, u32[]{:S(2)}) collective-permute-start(bf16[32,1,512]{2,0,1:T(8,128)(2,1)} %param.4), channel_id=1, source_target_pairs={{0,16},{16,32},{32,48},{48,64},{64,80},{80,96},{96,112},{112,128},... | collective-permute-start | bytes 98312 | tf_op jit(solution)/shard_map/ppermute | solution.py:15
  11.2 6.0 %collective-permute-start.1 = (bf16[32,1,512]{2,0,1:T(8,128)(2,1)}, bf16[32,1,512]{2,0,1:T(8,128)(2,1)S(1)}, u32[]{:S(2)}, u32[]{:S(2)}) collective-permute-start(bf16[32,1,512]{2,0,1:T(8,128)(2,1)} %param.4), channel_id=1, source_target_pairs={{16,0},{32,16},{48,32},{64,48},{80,64},{96,80},{112,96},{128,112},... | collective-permute-start | bytes 98312 | tf_op jit(solution)/shard_map/ppermute | solution.py:17
  18.6 143.6 %all-gather.5.cloned.1.call-start = ((), (), s32[]{:S(2)}) async-start(), calls=%async_computation.2 | async-start | bytes 1671168 | tf_op jit(solution)/shard_map/all_gather | solution.py:83
  84.9 4.1 copy-start
  89.5 72.8 %copy-start.2 = (bf16[32,3,3,512]{3,0,2,1:T(8,128)(2,1)S(1)}, bf16[32,3,3,512]{3,0,2,1:T(8,128)(2,1)}, u32[]{:S(2)}) copy-start(bf16[32,3,3,512]{3,0,2,1:T(8,128)(2,1)} %param.6) | copy-start | bytes 884740
  90.9 5.0 collective-permute-start.2
  94.4 5.8 %collective-permute-start.3 = (bf16[32,1,512]{2,0,1:T(8,128)(2,1)S(1)}, bf16[32,1,512]{2,0,1:T(8,128)(2,1)S(1)}, u32[]{:S(2)}, u32[]{:S(2)}) collective-permute-start(bf16[32,1,512]{2,0,1:T(8,128)(2,1)S(1)} %get-tuple-element.9), channel_id=1, source_target_pairs={{16,0},{32,16},{48,32},{64,48},{80,64},{96,80},{112,96},{128,112},... | collective-permute-start | bytes 98312 | tf_op jit(solution)/shard_map/ppermute | solution.py:17
  100.9 169.5 %reduce-scatter.2.cloned.1.call-start = ((), (), s32[]{:S(2)}) async-start(), calls=%async_computation.3 | async-start | bytes 1114112 | tf_op jit(solution)/shard_map/reduce_scatter | solution.py:97
  162.2 4.1 copy-start.1
  166.5 0.8 copy-start.6
  166.7 1.5 copy-start.7
  168.3 7.2 %collective-permute-start.4 = (bf16[32,1,512]{2,0,1:T(8,128)(2,1)S(1)}, bf16[32,1,512]{2,0,1:T(8,128)(2,1)S(1)}, u32[]{:S(2)}, u32[]{:S(2)}) collective-permute-start(bf16[32,1,512]{2,0,1:T(8,128)(2,1)S(1)} %select_convert_fusion.1), channel_id=1, source_target_pairs={{16,0},{32,16},{48,32},{64,48},{80,64},{96,80},{112,96},{128,112},... | collective-permute-start | bytes 98312 | tf_op jit(solution)/shard_map/ppermute | solution.py:17
  169.6 6.6 %collective-permute-start.5 = (bf16[32,1,512]{2,0,1:T(8,128)(2,1)S(1)}, bf16[32,1,512]{2,0,1:T(8,128)(2,1)S(1)}, u32[]{:S(2)}, u32[]{:S(2)}) collective-permute-start(bf16[32,1,512]{2,0,1:T(8,128)(2,1)S(1)} %select_convert_fusion.1), channel_id=1, source_target_pairs={{0,16},{16,32},{32,48},{48,64},{64,80},{80,96},{96,112},{112,128},... | collective-permute-start | bytes 98312 | tf_op jit(solution)/shard_map/ppermute | solution.py:15
  180.0 354.4 %all-reduce.25.cloned.1.call-start = ((), (), s32[]{:S(2)}) async-start(), calls=%async_computation.4 | async-start | bytes 2359296 | tf_op jit(solution)/shard_map/psum | solution.py:101
  181.9 88.5 %copy-start.5 = (f32[32,1,512]{2,0,1:T(8,128)S(1)}, f32[32,1,512]{2,0,1:T(8,128)}, u32[]{:S(2)}) copy-start(f32[32,1,512]{2,0,1:T(8,128)} %get-tuple-element.10) | copy-start | bytes 196612
  534.3 2.0 copy-start.3
Sparse Core Ops, SparseCore 0:
  18.8 66.1 all-gather.2
  101.0 61.2 all-gather.4
  180.1 90.2 reduce-scatter.1
  274.8 259.5 all-reduce.24
where the time goes:
time: 544 us
  waiting for transfers between devices  484 us (89%)
  matrix products  20.8 us (4%)
  starting transfers between devices  16 us (3%)
  between operations  14 us (3%)
    psum x1, waiting for transfers between devices, per_device(): first_grad, second_grad = lax.psum((first_local, second_local), 'rows')  260 us
    all_gather x2, waiting for transfers between devices, all_channels(): return lax.all_gather(with_rims(value), 'filt', axis=0, tiled=True)  128 us
    reduce_scatter x1, waiting for transfers between devices, per_device(): lax.psum_scatter(terms, 'filt', scatter_dimension=0, tiled=True)  87 us
    ppermute x3, starting transfers between devices, extended(): lax.ppermute(tail, axis, [(i, (i + 1) % count) for i in range(ends)])  12 us
    dot_general x18, matrix products, conv_forward(): jnp.einsum('oi,ihw->ohw', weight[:, a, b, :], padded[:, a:a + count, :],...  11.3 us
  transfers between devices with their start and end apart: 10, of which 8 were waited for; matrix products, arithmetic and copies ran while one was open for 1% of the time, Pallas kernels for 0%

commit v1 on v0

--- a/solution.py
+++ b/solution.py
@@ -80,7 +80,9 @@
 
 
 def all_channels(value):
-    return lax.all_gather(with_rims(value), "filt", axis=0, tiled=True)
+    return jnp.concatenate(
+        lax.all_to_all(jnp.stack([with_rims(value)] * lax.axis_size("filt")), "filt", 0, 0), axis=0
+    )
 
 
 def per_device(features, first_weight, second_weight, out_grad):

time: 544 us -> 469 us (0.86)
  waiting for transfers between devices: 484 us -> 360 us
  blocking collectives: 0 us -> 53.2 us
  matrix products: 20.8 us -> 13.7 us
    all_gather x2 -> x0, waiting for transfers between devices: 128 us -> none  [all_channels(): return lax.all_gather(with_rims(value), 'filt', axis=0, tiled=True)]
    all_to_all x0 -> x2, blocking collectives: none -> 53.2 us  [all_channels(): lax.all_to_all(jnp.stack([with_rims(value)] * lax.axis_size('filt')), 'fi...]
    dot_general x18, matrix products: 11.3 us -> 4.2 us  [conv_forward(): jnp.einsum('oi,ihw->ohw', weight[:, a, b, :], padded[:, a:a + count, :],...]
  transfers between devices with their start and end apart: 10 -> 8, of which waited for: 8 -> 6; matrix products, arithmetic and copies ran while one was open for 1% -> 1% of each run, Pallas kernels for 0% -> 0%
where the time goes in v1:
time: 469 us
  waiting for transfers between devices  360 us (77%)
  blocking collectives  53.2 us (11%)
  starting transfers between devices  17.4 us (4%)
  between operations  14.3 us (3%)
  matrix products  13.7 us (3%)
  local copies, waits for them, and re-layouts  6.76 us (1%)
    psum x1, waiting for transfers between devices, per_device(): first_grad, second_grad = lax.psum((first_local, second_local), 'rows')  259 us
    reduce_scatter x1, waiting for transfers between devices, per_device(): lax.psum_scatter(terms, 'filt', scatter_dimension=0, tiled=True)  90 us
    all_to_all x2, blocking collectives, all_channels(): lax.all_to_all(jnp.stack([with_rims(value)] * lax.axis_size('filt')), 'fi...  53.2 us
    ppermute x3, starting transfers between devices, extended(): lax.ppermute(tail, axis, [(i, (i + 1) % count) for i in range(ends)])  13.4 us
    ppermute x3, waiting for transfers between devices, extended(): lax.ppermute(head, axis, [((i + 1) % count, i) for i in range(ends)])  9.51 us
  transfers between devices with their start and end apart: 8, of which 6 were waited for; matrix products, arithmetic and copies ran while one was open for 1% of the time, Pallas kernels for 0%

profile of v1, /device:TPU:2, one launch (start us, length us, event | category | flops | bytes accessed | tf_op | source)
XLA Modules:
  0.0 468.6 jit_solution(13412460129985256843)
XLA Ops:
  7.2 3.8 collective-permute-start
  11.0 1.3 collective-permute-start.1
  12.3 0.6 collective-permute-done
  12.9 4.1 collective-permute-done.1
  17.1 0.8 pad_maximum_fusion.2
  18.0 27.2 %all_to_all.10 = bf16[16,32,3,512]{3,1,2,0:T(8,128)(2,1)S(1)} all-to-all(bf16[16,32,3,512]{3,1,2,0:T(8,128)(2,1)S(1)} %stack.134), channel_id=1, replica_groups=mesh['rows'=32,'filt'=16] {'filt'}, dimensions={0} | all-to-all | bytes 3145728 | tf_op jit(solution)/shard_map/all_to_all | solution.py:84
  45.4 0.9 copy-done.2
  48.3 3.8 collective-permute-start.2
  52.1 1.3 collective-permute-start.3
  53.4 0.5 collective-permute-done.2
  53.9 5.4 %collective-permute-done.3 = bf16[32,1,512]{2,0,1:T(8,128)(2,1)S(1)} collective-permute-done((bf16[32,1,512]{2,0,1:T(8,128)(2,1)S(1)}, bf16[32,1,512]{2,0,1:T(8,128)(2,1)S(1)}, u32[]{:S(2)}, u32[]{:S(2)}) %collective-permute-start.3) | collective-permute-done | bytes 32800 | tf_op jit(solution)/shard_map/ppermute | solution.py:17
  59.5 25.9 %all_to_all.11 = bf16[16,32,3,512]{3,1,2,0:T(8,128)(2,1)S(1)} all-to-all(bf16[16,32,3,512]{3,1,2,0:T(8,128)(2,1)S(1)} %stack.135), channel_id=1, replica_groups=mesh['rows'=32,'filt'=16] {'filt'}, dimensions={0} | all-to-all | bytes 3145728 | tf_op jit(solution)/shard_map/all_to_all | solution.py:84
  85.5 0.9 copy-done
  88.3 0.8 maximum_convert_fusion
  89.2 1.3 collective-permute-start.4
  90.5 5.8 %collective-permute-start.5 = (bf16[32,1,512]{2,0,1:T(8,128)(2,1)S(1)}, bf16[32,1,512]{2,0,1:T(8,128)(2,1)S(1)}, u32[]{:S(2)}, u32[]{:S(2)}) collective-permute-start(bf16[32,1,512]{2,0,1:T(8,128)(2,1)S(1)} %select_convert_fusion.1), channel_id=1, source_target_pairs={{0,16},{16,32},{32,48},{48,64},{64,80},{80,96},{96,112},{112,128},... | collective-permute-start | bytes 98312 | tf_op jit(solution)/shard_map/ppermute | solution.py:15
  96.2 0.3 convolution_bitcast_fusion.5
  96.6 0.3 convolution_bitcast_fusion.3
  96.9 0.3 convolution_bitcast_fusion.4
  97.3 0.3 slice.251
  97.6 0.3 convolution_bitcast_fusion.8
  98.0 0.3 slice.249
  98.3 0.3 convolution_bitcast_fusion.2
  98.6 0.3 slice.253
  99.0 0.3 convolution_bitcast_fusion
  99.3 0.3 convolution_bitcast_fusion.6
  99.7 0.3 convolution_bitcast_fusion.7
  100.0 2.0 fusion.1
  102.3 0.3 convolution_bitcast_fusion.29
  102.6 0.3 convolution_bitcast_fusion.28
  103.1 0.3 convolution_bitcast_fusion.32
  103.7 0.3 convolution_bitcast_fusion.35
  104.0 0.3 convolution_bitcast_fusion.31
  104.2 0.3 convolution_bitcast_fusion.34
  104.6 0.9 pad_maximum_fusion.1
  105.4 90.0 %reduce-scatter.2.cloned.1.call-done = f32[32,1,512]{2,0,1:T(8,128)} async-done(((f32[512,1,512]{2,0,1:T(8,128)}), f32[32,1,512]{2,0,1:T(8,128)}) %reduce-scatter.2.cloned.1.call-update) | async-done | bytes 65552 | tf_op jit(solution)/shard_map/reduce_scatter | solution.py:99
  195.4 0.8 select_convert_fusion
  196.6 0.3 convolution_bitcast_fusion.41
  196.8 0.3 convolution_bitcast_fusion.44
  197.1 0.3 convolution_bitcast_fusion.43
  197.4 0.3 convolution_bitcast_fusion.39
  197.6 0.3 convolution_bitcast_fusion.42
  197.9 0.3 convolution_bitcast_fusion.38
  198.2 0.3 convolution_bitcast_fusion.37
  198.8 0.9 pad_maximum_fusion
  199.7 259.3 %all-reduce.25.cloned.1.call-done = (f32[32,3,3,512]{3,0,2,1:T(8,128)}, f32[32,3,3,512]{3,0,2,1:T(8,128)}) async-done(((f32[32,3,3,512]{3,0,2,1:T(8,128)}, f32[32,3,3,512]{3,0,2,1:T(8,128)}), (f32[32,3,3,512]{3,0,2,1:T(8,128)}, f32[32,3,3,512]{3,0,2,1:T(8,128)})) %all-reduce.25.cloned.1.call-update) | async-done | bytes 1179664 | tf_op jit(solution)/shard_map/psum | solution.py:103
  459.0 2.0 copy.49
  461.0 0.8 copy.50
  (54 shorter events, 6.2 us)
Async XLA Ops:
  7.2 188.2 %reduce-scatter.2.cloned.1.call-start = ((), (), s32[]{:S(2)}) async-start(), calls=%async_computation.3 | async-start | bytes 1114112 | tf_op jit(solution)/shard_map/reduce_scatter | solution.py:99
  7.2 5.7 %collective-permute-start = (bf16[32,1,512]{2,0,1:T(8,128)(2,1)}, bf16[32,1,512]{2,0,1:T(8,128)(2,1)S(1)}, u32[]{:S(2)}, u32[]{:S(2)}) collective-permute-start(bf16[32,1,512]{2,0,1:T(8,128)(2,1)} %param.4), channel_id=1, source_target_pairs={{0,16},{16,32},{32,48},{48,64},{64,80},{80,96},{96,112},{112,128},... | collective-permute-start | bytes 98312 | tf_op jit(solution)/shard_map/ppermute | solution.py:15
  11.0 6.0 %collective-permute-start.1 = (bf16[32,1,512]{2,0,1:T(8,128)(2,1)}, bf16[32,1,512]{2,0,1:T(8,128)(2,1)S(1)}, u32[]{:S(2)}, u32[]{:S(2)}) collective-permute-start(bf16[32,1,512]{2,0,1:T(8,128)(2,1)} %param.4), channel_id=1, source_target_pairs={{16,0},{32,16},{48,32},{64,48},{80,64},{96,80},{112,96},{128,112},... | collective-permute-start | bytes 98312 | tf_op jit(solution)/shard_map/ppermute | solution.py:17
  45.3 1.0 copy-start.2
  48.3 5.6 %collective-permute-start.2 = (bf16[32,1,512]{2,0,1:T(8,128)(2,1)S(1)}, bf16[32,1,512]{2,0,1:T(8,128)(2,1)S(1)}, u32[]{:S(2)}, u32[]{:S(2)}) collective-permute-start(bf16[32,1,512]{2,0,1:T(8,128)(2,1)S(1)} %get-tuple-element.9), channel_id=1, source_target_pairs={{0,16},{16,32},{32,48},{48,64},{64,80},{80,96},{96,112},{112,128},... | collective-permute-start | bytes 98312 | tf_op jit(solution)/shard_map/ppermute | solution.py:15
  52.1 7.1 %collective-permute-start.3 = (bf16[32,1,512]{2,0,1:T(8,128)(2,1)S(1)}, bf16[32,1,512]{2,0,1:T(8,128)(2,1)S(1)}, u32[]{:S(2)}, u32[]{:S(2)}) collective-permute-start(bf16[32,1,512]{2,0,1:T(8,128)(2,1)S(1)} %get-tuple-element.9), channel_id=1, source_target_pairs={{16,0},{32,16},{48,32},{64,48},{80,64},{96,80},{112,96},{128,112},... | collective-permute-start | bytes 98312 | tf_op jit(solution)/shard_map/ppermute | solution.py:17
  85.4 1.0 copy-start
  87.2 1.1 copy-start.3
  87.6 1.5 copy-start.4
  89.2 8.4 %collective-permute-start.4 = (bf16[32,1,512]{2,0,1:T(8,128)(2,1)S(1)}, bf16[32,1,512]{2,0,1:T(8,128)(2,1)S(1)}, u32[]{:S(2)}, u32[]{:S(2)}) collective-permute-start(bf16[32,1,512]{2,0,1:T(8,128)(2,1)S(1)} %select_convert_fusion.1), channel_id=1, source_target_pairs={{16,0},{32,16},{48,32},{64,48},{80,64},{96,80},{112,96},{128,112},... | collective-permute-start | bytes 98312 | tf_op jit(solution)/shard_map/ppermute | solution.py:17
  90.5 7.8 %collective-permute-start.5 = (bf16[32,1,512]{2,0,1:T(8,128)(2,1)S(1)}, bf16[32,1,512]{2,0,1:T(8,128)(2,1)S(1)}, u32[]{:S(2)}, u32[]{:S(2)}) collective-permute-start(bf16[32,1,512]{2,0,1:T(8,128)(2,1)S(1)} %select_convert_fusion.1), channel_id=1, source_target_pairs={{0,16},{16,32},{32,48},{48,64},{64,80},{80,96},{96,112},{112,128},... | collective-permute-start | bytes 98312 | tf_op jit(solution)/shard_map/ppermute | solution.py:15
  102.0 356.9 %all-reduce.25.cloned.1.call-start = ((), (), s32[]{:S(2)}) async-start(), calls=%async_computation.4 | async-start | bytes 2359296 | tf_op jit(solution)/shard_map/psum | solution.py:103
  459.0 2.0 copy-start.1
Sparse Core Ops, SparseCore 0:
  102.2 93.1 reduce-scatter.1
  199.8 259.1 all-reduce.24
